TPU v7x, 256 devices: a whole 4x4x8 slice. The times are simulated.
256 devices in a mesh: sec: 32 (over z, y), depth: 4 (over x), segment: 2 (over core).
Axes of the slice: x: 4, y: 4, z: 8, core: 2. Of those that a mesh axis runs over, the one named last changes fastest.
Arguments:
- fields: float32 [2, 9, 64, 64, 128], P('segment', None, 'sec', 'depth'), may hold values from -6 to 6
- block_ids: int32 [2, 64, 64, 128], P('segment', 'sec', 'depth'), may hold values from 0 to 15
- buoyancy: float32 [16], replicated, may hold values from 0.5 to 1
- lame_lambda: float32 [16], replicated, may hold values from 0.2 to 0.6
- lame_mu: float32 [16], replicated, may hold values from 0.1 to 0.3
- moments: float32 [6, 131072], P(None, ('sec', 'depth')), may hold values from -12 to 12
- moment_owner: int32 [131072, 1], P(('sec', 'depth')), may hold values from 0 to 31; in each aligned block of 1024 rows (0 to 1023, 1024 to 2047, ...) at most 64 rows name the same one
- moment_cells: int32 [131072], P(('sec', 'depth')), may hold values from 0 to 4095
- drm_rows: int32 [262144], P(('sec', 'depth')), may hold values from 0 to 4095
Outputs:
- final_fields: float32 [2, 9, 64, 64, 128], P('segment', None, 'sec', 'depth')
Inputs may be any that keep to these rules, and one draw needn't show every extreme that they name: `moment_owner`: in the entries of one section and slab at most 64 name the same section, a bound that some block reaches of them.
All inputs are finite; a program needn't handle non-finite values.
Results may differ from a plain program's by a relative error of at most 0.00002.
Values sent between devices are 32-bit elements; how exact they have to be, the bound alone decides.
A program may use at most 64 MiB of HBM per device.

v0:
```python
import jax
import jax.numpy as jnp
from jax import lax
from jax.sharding import PartitionSpec as P

STEPS = 4
HALF_STEP = 0.5


def passed_along(block, axis, distance):
    devices = range(lax.axis_size(axis))
    route = [(i - distance, i) for i in devices if i - distance in devices]
    return lax.ppermute(block, axis, route)


def lookup(block_ids, table):
    result = jnp.zeros(block_ids.shape, jnp.float32)
    for entry in range(table.shape[0]):
        result = result + jnp.where(block_ids == entry, table[entry], jnp.float32(0.0))
    return result


def back_diff(field, before_rim, axis):
    count = field.shape[axis]
    before = jnp.concatenate([before_rim, lax.slice_in_dim(field, 0, count - 1, axis=axis)], axis)
    return field - before


def fore_diff(field, after_rim, axis):
    count = field.shape[axis]
    after = jnp.concatenate([lax.slice_in_dim(field, 1, count, axis=axis), after_rim], axis)
    return after - field


def stress_rims(state):
    xplane = jnp.stack([state[:, 3, -1:], state[:, 8, -1:], state[:, 7, -1:]], axis=1)
    zplane = jnp.stack([state[:, 7, :, -1:], state[:, 6, :, -1:], state[:, 5, :, -1:]], axis=1)
    x_rims = passed_along(xplane, "sec", 1)
    z_rims = passed_along(zplane, "depth", 1)
    return (x_rims, z_rims)


def velocity_rims(newv):
    xplane = newv[:, :, :1]
    zplane = newv[:, :, :, :1]
    x_rims = passed_along(xplane, "sec", -1)
    z_rims = passed_along(zplane, "depth", -1)
    return (x_rims, z_rims)


def couple(newv, oldv, rows_here):
    shape_one = newv.shape[1:]
    increment = (newv[0] - oldv[0]).reshape(3, -1)[:, rows_here]
    arrived = passed_along(increment, "segment", 1)
    basin = newv[0].reshape(3, -1).at[:, rows_here].add(arrived)
    return basin.reshape((1,) + shape_one)


def advance(state, buoy, lam, shear, rows_here):
    x_rims, z_rims = stress_rims(state)
    vx, vy, vz = (state[:, 0], state[:, 1], state[:, 2])
    sxx, syy, szz, syz, sxz, sxy = (state[:, k] for k in range(3, 9))
    y_zero = jnp.zeros_like(sxx[..., :1])
    nvx = vx + HALF_STEP * buoy * (
        back_diff(sxx, x_rims[:, 0], 1)
        + back_diff(sxy, y_zero, 3)
        + back_diff(sxz, z_rims[:, 0], 2)
    )
    nvy = vy + HALF_STEP * buoy * (
        back_diff(sxy, x_rims[:, 1], 1)
        + back_diff(syy, y_zero, 3)
        + back_diff(syz, z_rims[:, 1], 2)
    )
    nvz = vz + HALF_STEP * buoy * (
        back_diff(sxz, x_rims[:, 2], 1)
        + back_diff(syz, y_zero, 3)
        + back_diff(szz, z_rims[:, 2], 2)
    )
    newv = couple(jnp.stack([nvx, nvy, nvz], axis=1), state[:, :3], rows_here)
    vx_rims, vz_rims = velocity_rims(newv)
    vx, vy, vz = (newv[:, 0], newv[:, 1], newv[:, 2])
    exx = fore_diff(vx, vx_rims[:, 0], 1)
    eyy = fore_diff(vy, y_zero, 3)
    ezz = fore_diff(vz, vz_rims[:, 2], 2)
    trace = exx + eyy + ezz
    sxx = sxx + HALF_STEP * (lam * trace + 2.0 * shear * exx)
    syy = syy + HALF_STEP * (lam * trace + 2.0 * shear * eyy)
    szz = szz + HALF_STEP * (lam * trace + 2.0 * shear * ezz)
    syz = syz + HALF_STEP * shear * (fore_diff(vy, vz_rims[:, 1], 2) + fore_diff(vz, y_zero, 3))
    sxz = sxz + HALF_STEP * shear * (
        fore_diff(vx, vz_rims[:, 0], 2) + fore_diff(vz, vx_rims[:, 2], 1)
    )
    sxy = sxy + HALF_STEP * shear * (fore_diff(vx, y_zero, 3) + fore_diff(vy, vx_rims[:, 1], 1))
    return jnp.stack([vx, vy, vz, sxx, syy, szz, syz, sxz, sxy], axis=1)


def on_device(
    fields, block_ids, buoyancy, lame_lambda, lame_mu, moments, moment_owner, moment_cells, drm_rows
):
    my_section = lax.axis_index("sec")
    segment_pos = lax.axis_index("segment")
    width_x, width_z, width_y = (fields.shape[2], fields.shape[3], fields.shape[4])
    cells_here = width_x * width_z * width_y
    all_moments, all_owner, all_cells = (
        lax.all_gather(moments, "sec", axis=1, tiled=True),
        lax.all_gather(moment_owner, "sec", axis=0, tiled=True),
        lax.all_gather(moment_cells, "sec", axis=0, tiled=True),
    )
    values = all_moments
    places = jnp.where(all_owner[:, 0] == my_section, all_cells, cells_here)
    values = values * (segment_pos == 0).astype(jnp.float32)
    stress = fields[0, 3:].reshape(6, -1).at[:, places].add(values, mode="drop")
    state = jnp.concatenate(
        [fields[:, :3], stress.reshape(1, 6, width_x, width_z, width_y)], axis=1
    )
    block_here = block_ids[:, None]
    block_here = block_here[:, 0]
    buoy = lookup(block_here, buoyancy)
    lam = lookup(block_here, lame_lambda)
    shear = lookup(block_here, lame_mu)
    for step in range(STEPS):
        state = advance(state, buoy, lam, shear, drm_rows)
    return state


def solution(mesh):
    in_specs = (
        P("segment", None, "sec", "depth", None),
        P("segment", "sec", "depth", None),
        P(),
        P(),
        P(),
        P(None, ("sec", "depth")),
        P(("sec", "depth"), None),
        P(("sec", "depth")),
        P(("sec", "depth")),
    )
    out_specs = P("segment", None, "sec", "depth", None)
    return jax.shard_map(
        on_device, mesh=mesh, in_specs=in_specs, out_specs=out_specs, check_vma=False
    )
```

profile of v0, /device:TPU:124, one launch (start us, length us, event | category | flops | bytes accessed | tf_op | source)
XLA Modules:
  0.0 604.5 jit_solution(15526155525644759450)
XLA Ops:
  0.0 49.8 %all_gather.11 = f32[6,32768]{1,0:T(8,128)S(1)} all-gather(f32[6,1024]{1,0:T(8,128)} %param.14), channel_id=1, replica_groups=mesh['sec'=32,'depth'=4,'segment'=2] {'sec'}, dimensions={1}, use_global_device_ids=true | all-gather | bytes 811008 | tf_op jit(solution)/shard_map/all_gather | solution.py:105
  50.0 8.9 %copy.799 = f32[32768,6]{1,0:T(8,128)} copy(f32[32768,6]{0,1:T(8,128)S(1)} %multiply_bitcast_fusion) | data formatting | bytes 1572864 | tf_op jit(solution)/shard_map/mul | solution.py:111
  58.9 41.3 %all_gather.9 = s32[32768,1]{0,1:T(1,128)S(1)} all-gather(s32[1024,1]{0,1:T(1,128)S(1)} %copy-done.12), channel_id=1, replica_groups=mesh['sec'=32,'depth'=4,'segment'=2] {'sec'}, dimensions={0}, use_global_device_ids=true | all-gather | bytes 135168 | tf_op jit(solution)/shard_map/all_gather | solution.py:106
  100.1 42.0 %all_gather.10 = s32[32768]{0:T(1024)S(1)} all-gather(s32[1024]{0:T(1024)S(1)} %copy-done.13), channel_id=1, replica_groups=mesh['sec'=32,'depth'=4,'segment'=2] {'sec'}, dimensions={0}, use_global_device_ids=true | all-gather | bytes 135168 | tf_op jit(solution)/shard_map/all_gather | solution.py:107
  143.2 175.0 %scatter_fusion = f32[6,4096]{0,1:T(8,128)S(1)} fusion(f32[6,4096]{0,1:T(8,128)S(1)} %bitcast.376, s32[32768]{0:T(1024)S(1)} %compare_select_fusion, f32[32768,6]{1,0:T(8,128)} %copy.799), kind=kCustom, calls=%fused_computation.4 | custom fusion | flops 196608 | bytes 2490368 | tf_op jit(solution)/shard_map/scatter-add | solution.py:112
  318.7 3.1 collective-permute-start.1
  327.3 4.7 collective-permute-start
  332.0 7.3 %fusion.93 = (f32[1,1,2,16,128]{1,4,3,2,0:T(8,128)}, f32[1,1,2,16,128]{1,4,3,2,0:T(8,128)}, f32[1,1,2,16,128]{1,4,3,2,0:T(8,128)}, f32[1,1,2,16,128]{1,4,3,2,0:T...) fusion(f32[1,6,2,16,128]{1,4,3,2,0:T(8,128)S(1)} %bitcast.379), kind=kLoop, calls=%fused_computation.240 | loop fusion | bytes 196608 | tf_op jit(solution)/shard_map/slice | solution.py:62
  340.8 2.4 copy.866
  343.2 2.2 copy.865
  346.0 2.4 copy.871
  348.4 2.2 copy.870
  353.3 10.7 %fusion.3 = (f32[1,2,16,128]{3,2,1,0:T(8,128)S(1)}, f32[1,2,16,128]{3,2,1,0:T(8,128)S(1)}, pred[1,2,16,128]{3,2,1,0:T(8,128)(4,1)S(1)}, pred[1,2,16,128]{3,2,1,0...) fusion(f32[1,1,16,128]{3,2,1,0:T(8,128)S(1)} %slice.912, ...), kind=kLoop, calls=%fused_computation.29 | loop fusion | flops 233472 | bytes 229312 | tf_op jit(solution)/shard_map/add | solution.py:64
  364.8 3.2 bitcast_subtract_fusion
  367.9 7.0 %gather_fusion = f32[2048,3]{1,0:T(8,128)S(1)} fusion(f32[3,4096]{0,1:T(8,128)} %bitcast_subtract_fusion, s32[2048]{0:T(1024)S(1)} %get-tuple-element.103), kind=kCustom, calls=%fused_computation | custom fusion | bytes 57344 | tf_op jit(solution)/shard_map/gather | solution.py:53
  377.9 12.2 %scatter_fusion.1 = f32[3,4096]{0,1:T(8,128)S(1)} fusion(f32[3,4096]{0,1:T(8,128)S(1)} %copy.807, s32[2048]{0:T(1024)S(1)} %get-tuple-element.104, f32[2048,3]{1,0:T(8,128)S(1)} %copy.808), kind=kCustom, calls=%fused_computation.5 | custom fusion | flops 6144 | bytes 81920 | tf_op jit(solution)/shard_map/scatter-add | solution.py:55
  390.2 2.7 collective-permute-start.4
  393.0 4.0 fusion.92
  399.3 2.2 copy.876
  406.2 7.1 %collective-permute-done.3 = f32[1,3,1,16,128]{4,3,2,1,0:T(8,128)S(1)} collective-permute-done((f32[1,3,1,16,128]{4,3,2,1,0:T(8,128)S(1)}, f32[1,3,1,16,128]{4,3,2,1,0:T(8,128)S(1)}, u32[]{:S(2)}, u32[]{:S(2)}) %collective-permute-start.3) | collective-permute-done | bytes 24608 | tf_op jit(solution)/shard_map/ppermute | solution.py:13
  413.3 20.5 %multiply_add_fusion.6 = (f32[1,2,16,128]{3,2,1,0:T(8,128)S(1)}, f32[1,2,16,128]{3,2,1,0:T(8,128)S(1)}, f32[1,2,16,128]{3,2,1,0:T(8,128)S(1)}, f32[1,2,16,128]{3,2,1,0:T(8,128)S(1)}) fusion(f32[1,2,16,127]{3,2,1,0:T(8,128)S(1)} %slice.939, f32[1,1,2,16,128]{4,3,2,1,0:T(8,128)S(1)} %copy.875, f32[1,1,2,16,128]{4,3,2,1,0:T(8,128)S(1)} %copy.870, ...), kind=kLoop, calls=%fused_computation.178 | loop fusion | flops 307200 | bytes 245760 | tf_op jit(solution)/shard_map/add | solution.py:87
  433.9 3.1 collective-permute-start.6
  439.4 3.4 collective-permute-done.5
  445.0 3.2 sub.500
  448.2 7.2 %gather_fusion.1 = f32[2048,3]{1,0:T(8,128)S(1)} fusion(f32[3,4096]{0,1:T(8,128)} %sub.500, s32[2048]{0:T(1024)S(1)} %get-tuple-element.103), kind=kCustom, calls=%fused_computation.1 | custom fusion | bytes 57344 | tf_op jit(solution)/shard_map/gather | solution.py:53
  458.2 12.2 %scatter_fusion.2 = f32[3,4096]{0,1:T(8,128)S(1)} fusion(f32[3,4096]{0,1:T(8,128)S(1)} %copy-done, s32[2048]{0:T(1024)S(1)} %get-tuple-element.104, f32[2048,3]{1,0:T(8,128)S(1)} %copy.821), kind=kCustom, calls=%fused_computation.6 | custom fusion | flops 6144 | bytes 81920 | tf_op jit(solution)/shard_map/scatter-add | solution.py:55
  470.6 2.7 collective-permute-start.9
  473.3 4.0 fusion.91
  479.6 2.2 copy.883
  481.9 2.2 copy.881
  486.6 7.1 %collective-permute-done.8 = f32[1,3,1,16,128]{4,3,2,1,0:T(8,128)S(1)} collective-permute-done((f32[1,3,1,16,128]{4,3,2,1,0:T(8,128)S(1)}, f32[1,3,1,16,128]{4,3,2,1,0:T(8,128)S(1)}, u32[]{:S(2)}, u32[]{:S(2)}) %collective-permute-start.8) | collective-permute-done | bytes 24608 | tf_op jit(solution)/shard_map/ppermute | solution.py:13
  493.8 3.1 collective-permute-start.11
  499.3 3.4 collective-permute-done.10
  504.9 3.2 sub.519
  508.1 7.2 %gather_fusion.2 = f32[2048,3]{1,0:T(8,128)S(1)} fusion(f32[3,4096]{0,1:T(8,128)} %sub.519, s32[2048]{0:T(1024)S(1)} %get-tuple-element.103), kind=kCustom, calls=%fused_computation.2 | custom fusion | bytes 57344 | tf_op jit(solution)/shard_map/gather | solution.py:53
  518.1 12.2 %scatter_fusion.3 = f32[3,4096]{0,1:T(8,128)S(1)} fusion(f32[3,4096]{0,1:T(8,128)S(1)} %copy-done.1, s32[2048]{0:T(1024)S(1)} %get-tuple-element.104, f32[2048,3]{1,0:T(8,128)S(1)} %copy.834), kind=kCustom, calls=%fused_computation.7 | custom fusion | flops 6144 | bytes 81920 | tf_op jit(solution)/shard_map/scatter-add | solution.py:55
  530.5 2.8 collective-permute-start.14
  533.2 4.0 fusion.90
  539.5 2.2 copy.892
  541.8 2.2 copy.889
  546.5 7.1 %collective-permute-done.13 = f32[1,3,1,16,128]{4,3,2,1,0:T(8,128)S(1)} collective-permute-done((f32[1,3,1,16,128]{4,3,2,1,0:T(8,128)S(1)}, f32[1,3,1,16,128]{4,3,2,1,0:T(8,128)S(1)}, u32[]{:S(2)}, u32[]{:S(2)}) %collective-permute-start.13) | collective-permute-done | bytes 24608 | tf_op jit(solution)/shard_map/ppermute | solution.py:13
  553.7 3.1 collective-permute-start.16
  559.2 3.4 collective-permute-done.15
  564.8 3.2 sub.538
  568.0 7.2 %gather_fusion.3 = f32[2048,3]{1,0:T(8,128)S(1)} fusion(f32[3,4096]{0,1:T(8,128)} %sub.538, s32[2048]{0:T(1024)S(1)} %get-tuple-element.103), kind=kCustom, calls=%fused_computation.3 | custom fusion | bytes 57344 | tf_op jit(solution)/shard_map/gather | solution.py:53
  578.0 12.2 %scatter_fusion.4 = f32[3,4096]{0,1:T(8,128)S(1)} fusion(f32[3,4096]{0,1:T(8,128)S(1)} %copy-done.2, s32[2048]{0:T(1024)S(1)} %get-tuple-element.104, f32[2048,3]{1,0:T(8,128)S(1)} %copy.847), kind=kCustom, calls=%fused_computation.8 | custom fusion | flops 6144 | bytes 81920 | tf_op jit(solution)/shard_map/scatter-add | solution.py:55
  591.0 2.8 collective-permute-start.19
  596.5 6.6 %collective-permute-done.18 = f32[1,3,1,16,128]{4,3,2,1,0:T(8,128)S(1)} collective-permute-done((f32[1,3,1,16,128]{4,3,2,1,0:T(8,128)S(1)}, f32[1,3,1,16,128]{4,3,2,1,0:T(8,128)S(1)}, u32[]{:S(2)}, u32[]{:S(2)}) %collective-permute-start.18) | collective-permute-done | bytes 24608 | tf_op jit(solution)/shard_map/ppermute | solution.py:13
  (222 shorter events, 59.5 us)
Async XLA Ops:
  49.9 8.9 %copy-start.12 = (s32[1024,1]{0,1:T(1,128)S(1)}, s32[1024,1]{0,1:T(1,128)}, u32[]{:S(2)}) copy-start(s32[1024,1]{0,1:T(1,128)} %param.15) | copy-start | bytes 12292
  49.9 50.2 %copy-start.13 = (s32[1024]{0:T(1024)S(1)}, s32[1024]{0:T(1024)}, u32[]{:S(2)}) copy-start(s32[1024]{0:T(1024)} %param.16) | copy-start | bytes 12292
  49.9 92.2 %slice-start = ((f32[1,9,2,16,128]{4,3,2,1,0:T(8,128)}), f32[1,6,2,16,128]{4,3,2,1,0:T(8,128)S(1)}, s32[]{:S(2)}) async-start(f32[1,9,2,16,128]{4,3,2,1,0:T(8,128)} %param.9), calls=%async_computation | async-start | bytes 196608 | tf_op jit(solution)/shard_map/slice | solution.py:112
  318.7 34.6 %collective-permute-start.1 = (f32[1,3,2,1,128]{4,3,2,1,0:T(1,128)S(1)}, f32[1,3,2,1,128]{4,3,2,1,0:T(1,128)S(1)}, u32[]{:S(2)}, u32[]{:S(2)}) collective-permute-start(f32[1,3,2,1,128]{4,3,2,1,0:T(1,128)S(1)} %pad_maximum_fusion.8), channel_id=1, source_target_pairs={{0,2},{2,4},{4,6},{1,3},{3,5},{5,7},{8,10},{10,12},{12,14},{9,11},... | collective-permute-start | bytes 9224 | tf_op jit(solution)/shard_map/ppermute | solution.py:13
  327.2 12.1 %copy-start.6 = (f32[16]{0:T(128)S(1)}, f32[16]{0:T(128)}, u32[]{:S(2)}) copy-start(f32[16]{0:T(128)} %param.11) | copy-start | bytes 196
  327.2 12.8 %copy-start.11 = (s32[2048]{0:T(1024)S(1)}, s32[2048]{0:T(1024)}, u32[]{:S(2)}) copy-start(s32[2048]{0:T(1024)} %param.17) | copy-start | bytes 24580
  327.3 12.8 %copy-start.7 = (f32[16]{0:T(128)S(1)}, f32[16]{0:T(128)}, u32[]{:S(2)}) copy-start(f32[16]{0:T(128)} %param.12) | copy-start | bytes 196
  327.3 26.0 %collective-permute-start = (f32[1,3,1,16,128]{4,3,2,1,0:T(8,128)S(1)}, f32[1,3,1,16,128]{4,3,2,1,0:T(8,128)S(1)}, u32[]{:S(2)}, u32[]{:S(2)}) collective-permute-start(f32[1,3,1,16,128]{4,3,2,1,0:T(8,128)S(1)} %pad_maximum_fusion.4), channel_id=1, source_target_pairs={{0,8},{8,16},{16,24},{24,32},{32,40},{40,48},{48,56},{56,64},{64,7... | collective-permute-start | bytes 73736 | tf_op jit(solution)/shard_map/ppermute | solution.py:13
  340.8 4.6 copy-start.4
  346.0 4.6 copy-start.3
  348.4 2.9 slice-start.1
  350.6 2.7 copy-start.5
  350.6 2.7 copy-start.10
  364.8 12.0 %copy-start.8 = (f32[16]{0:T(128)S(1)}, f32[16]{0:T(128)}, u32[]{:S(2)}) copy-start(f32[16]{0:T(128)} %param.13) | copy-start | bytes 196
  375.3 2.2 collective-permute-start.2
  390.2 16.0 %collective-permute-start.4 = (f32[1,3,2,1,128]{4,2,3,1,0:T(2,128)S(1)}, f32[1,3,2,1,128]{4,2,3,1,0:T(2,128)S(1)}, u32[]{:S(2)}, u32[]{:S(2)}) collective-permute-start(f32[1,3,2,1,128]{4,2,3,1,0:T(2,128)S(1)} %copy.877), channel_id=1, source_target_pairs={{2,0},{4,2},{6,4},{3,1},{5,3},{7,5},{10,8},{12,10},{14,12},{11,9},... | collective-permute-start | bytes 9224 | tf_op jit(solution)/shard_map/ppermute | solution.py:13
  404.3 9.0 %collective-permute-start.3 = (f32[1,3,1,16,128]{4,3,2,1,0:T(8,128)S(1)}, f32[1,3,1,16,128]{4,3,2,1,0:T(8,128)S(1)}, u32[]{:S(2)}, u32[]{:S(2)}) collective-permute-start(f32[1,3,1,16,128]{4,3,2,1,0:T(8,128)S(1)} %copy.874), channel_id=1, source_target_pairs={{8,0},{16,8},{24,16},{32,24},{40,32},{48,40},{56,48},{64,56},{72,6... | collective-permute-start | bytes 73736 | tf_op jit(solution)/shard_map/ppermute | solution.py:13
  433.9 5.5 collective-permute-start.6
  437.1 5.7 collective-permute-start.5
  448.2 10.0 %copy-start = (f32[3,4096]{0,1:T(8,128)S(1)}, f32[3,4096]{0,1:T(8,128)}, u32[]{:S(2)}) copy-start(f32[3,4096]{0,1:T(8,128)} %copy.820) | copy-start | bytes 147460
  455.7 2.1 collective-permute-start.7
  470.6 16.0 %collective-permute-start.9 = (f32[1,3,2,1,128]{4,2,3,1,0:T(2,128)S(1)}, f32[1,3,2,1,128]{4,2,3,1,0:T(2,128)S(1)}, u32[]{:S(2)}, u32[]{:S(2)}) collective-permute-start(f32[1,3,2,1,128]{4,2,3,1,0:T(2,128)S(1)} %copy.885), channel_id=1, source_target_pairs={{2,0},{4,2},{6,4},{3,1},{5,3},{7,5},{10,8},{12,10},{14,12},{11,9},... | collective-permute-start | bytes 9224 | tf_op jit(solution)/shard_map/ppermute | solution.py:13
  484.6 9.0 %collective-permute-start.8 = (f32[1,3,1,16,128]{4,3,2,1,0:T(8,128)S(1)}, f32[1,3,1,16,128]{4,3,2,1,0:T(8,128)S(1)}, u32[]{:S(2)}, u32[]{:S(2)}) collective-permute-start(f32[1,3,1,16,128]{4,3,2,1,0:T(8,128)S(1)} %copy.882), channel_id=1, source_target_pairs={{8,0},{16,8},{24,16},{32,24},{40,32},{48,40},{56,48},{64,56},{72,6... | collective-permute-start | bytes 73736 | tf_op jit(solution)/shard_map/ppermute | solution.py:13
  493.8 5.5 collective-permute-start.11
  497.0 5.7 collective-permute-start.10
  508.1 10.0 %copy-start.1 = (f32[3,4096]{0,1:T(8,128)S(1)}, f32[3,4096]{0,1:T(8,128)}, u32[]{:S(2)}) copy-start(f32[3,4096]{0,1:T(8,128)} %copy.833) | copy-start | bytes 147460
  515.6 2.1 collective-permute-start.12
  530.5 16.0 %collective-permute-start.14 = (f32[1,3,2,1,128]{4,2,3,1,0:T(2,128)S(1)}, f32[1,3,2,1,128]{4,2,3,1,0:T(2,128)S(1)}, u32[]{:S(2)}, u32[]{:S(2)}) collective-permute-start(f32[1,3,2,1,128]{4,2,3,1,0:T(2,128)S(1)} %copy.893), channel_id=1, source_target_pairs={{2,0},{4,2},{6,4},{3,1},{5,3},{7,5},{10,8},{12,10},{14,12},{11,9},... | collective-permute-start | bytes 9224 | tf_op jit(solution)/shard_map/ppermute | solution.py:13
  544.5 9.0 %collective-permute-start.13 = (f32[1,3,1,16,128]{4,3,2,1,0:T(8,128)S(1)}, f32[1,3,1,16,128]{4,3,2,1,0:T(8,128)S(1)}, u32[]{:S(2)}, u32[]{:S(2)}) collective-permute-start(f32[1,3,1,16,128]{4,3,2,1,0:T(8,128)S(1)} %copy.890), channel_id=1, source_target_pairs={{8,0},{16,8},{24,16},{32,24},{40,32},{48,40},{56,48},{64,56},{72,6... | collective-permute-start | bytes 73736 | tf_op jit(solution)/shard_map/ppermute | solution.py:13
  553.7 5.5 collective-permute-start.16
  556.9 5.7 collective-permute-start.15
  568.0 10.0 %copy-start.2 = (f32[3,4096]{0,1:T(8,128)S(1)}, f32[3,4096]{0,1:T(8,128)}, u32[]{:S(2)}) copy-start(f32[3,4096]{0,1:T(8,128)} %copy.846) | copy-start | bytes 147460
  575.5 2.1 collective-permute-start.17
  591.0 5.5 collective-permute-start.19
  594.0 9.0 %collective-permute-start.18 = (f32[1,3,1,16,128]{4,3,2,1,0:T(8,128)S(1)}, f32[1,3,1,16,128]{4,3,2,1,0:T(8,128)S(1)}, u32[]{:S(2)}, u32[]{:S(2)}) collective-permute-start(f32[1,3,1,16,128]{4,3,2,1,0:T(8,128)S(1)} %slice.1059), channel_id=1, source_target_pairs={{8,0},{16,8},{24,16},{32,24},{40,32},{48,40},{56,48},{64,56},{72,6... | collective-permute-start | bytes 73736 | tf_op jit(solution)/shard_map/ppermute | solution.py:13
  603.2 0.7 copy-start.9
where the time goes:
time: 606 us; the launch traced here: 604 us
  other arithmetic  270 us (45%)
  blocking collectives  133 us (22%)
  local copies, waits for them, and re-layouts  111 us (18%)
  starting transfers between devices  47.1 us (8%)
  waiting for transfers between devices  42.1 us (7%)
    scatter-add x1, other arithmetic, on_device(): stress = fields[0, 3:].reshape(6, -1).at[:, places].add(values, mode='drop')  175 us
    all_gather x1, blocking collectives, on_device(): lax.all_gather(moments, 'sec', axis=1, tiled=True)  49.8 us
    scatter-add x4, other arithmetic, couple(): basin = newv[0].reshape(3, -1).at[:, rows_here].add(arrived)  49 us
    ppermute x20, starting transfers between devices, passed_along(): return lax.ppermute(block, axis, route)  47.1 us
    ppermute x20, waiting for transfers between devices, passed_along(): return lax.ppermute(block, axis, route)  42.1 us
    all_gather x1, blocking collectives, on_device(): lax.all_gather(moment_cells, 'sec', axis=0, tiled=True)  42 us
    all_gather x1, blocking collectives, on_device(): lax.all_gather(moment_owner, 'sec', axis=0, tiled=True)  41.3 us
    unnamed x57, local copies, waits for them, and re-layouts  36 us
  transfers between devices with their start and end apart: 20, of which 14 were waited for; matrix products, arithmetic and copies ran while one was open for 10% of the time, Pallas kernels for 0%

commit v1 on v0

--- a/solution.py
+++ b/solution.py
@@ -104,7 +104,9 @@
     all_moments, all_owner, all_cells = (
         lax.all_gather(moments, "sec", axis=1, tiled=True),
         lax.all_gather(moment_owner, "sec", axis=0, tiled=True),
-        lax.all_gather(moment_cells, "sec", axis=0, tiled=True),
+        jnp.concatenate(
+            lax.all_to_all(jnp.stack([moment_cells] * lax.axis_size("sec")), "sec", 0, 0), axis=0
+        ),
     )
     values = all_moments
     places = jnp.where(all_owner[:, 0] == my_section, all_cells, cells_here)

time: 606 us -> 574 us (0.947)
  blocking collectives: 133 us -> 90.5 us
  starting transfers between devices: 47.1 us -> 57.2 us
    all_gather x1 -> x0, blocking collectives: 42 us -> none  [on_device(): lax.all_gather(moment_cells, 'sec', axis=0, tiled=True)]
    all_to_all x0 -> x1, starting transfers between devices: none -> 10.1 us  [on_device(): lax.all_to_all(jnp.stack([moment_cells] * lax.axis_size('sec')), 'sec', 0...]
  transfers between devices with their start and end apart: 20 -> 21, of which waited for: 14 -> 14; matrix products, arithmetic and copies ran while one was open for 10% -> 11% of each run, Pallas kernels for 0% -> 0%
where the time goes in v1:
time: 574 us; the launch traced here: 572 us
  other arithmetic  270 us (47%)
  local copies, waits for them, and re-layouts  111 us (19%)
  blocking collectives  90.5 us (16%)
  starting transfers between devices  57.2 us (10%)
  waiting for transfers between devices  42.1 us (7%)
    scatter-add x1, other arithmetic, on_device(): stress = fields[0, 3:].reshape(6, -1).at[:, places].add(values, mode='drop')  175 us
    all_gather x1, blocking collectives, on_device(): lax.all_gather(moments, 'sec', axis=1, tiled=True)  49.3 us
    scatter-add x4, other arithmetic, couple(): basin = newv[0].reshape(3, -1).at[:, rows_here].add(arrived)  49 us
    ppermute x20, starting transfers between devices, passed_along(): return lax.ppermute(block, axis, route)  47.1 us
    ppermute x20, waiting for transfers between devices, passed_along(): return lax.ppermute(block, axis, route)  42.1 us
    all_gather x1, blocking collectives, on_device(): lax.all_gather(moment_owner, 'sec', axis=0, tiled=True)  41.2 us
    unnamed x57, local copies, waits for them, and re-layouts  34.8 us
    gather x8, local copies, waits for them, and re-layouts, couple(): increment = (newv[0] - oldv[0]).reshape(3, -1)[:, rows_here]  30 us
  transfers between devices with their start and end apart: 21, of which 14 were waited for; matrix products, arithmetic and copies ran while one was open for 11% of the time, Pallas kernels for 0%

profile of v1, /device:TPU:124, one launch (start us, length us, event | category | flops | bytes accessed | tf_op | source)
XLA Modules:
  0.0 572.2 jit_solution(10258744910689513217)
XLA Ops:
  1.4 10.1 %all-to-all-start = ((s32[32,1,1024]{2,1,0:T(1,128)}), s32[32,1,1024]{2,1,0:T(1,128)S(1)}, u32[]{:S(2)}, u32[]{:S(2)}) async-start(s32[32,1,1024]{2,1,0:T(1,128)} %stack.180), calls=%async_computation | async-start | bytes 262144 | tf_op jit(solution)/shard_map/all_to_all | solution.py:108
  11.5 49.3 %all_gather.7 = f32[6,32768]{1,0:T(8,128)S(1)} all-gather(f32[6,1024]{1,0:T(8,128)} %param.14), channel_id=1, replica_groups=mesh['sec'=32,'depth'=4,'segment'=2] {'sec'}, dimensions={1}, use_global_device_ids=true | all-gather | bytes 811008 | tf_op jit(solution)/shard_map/all_gather | solution.py:105
  60.9 8.9 %copy.799 = f32[32768,6]{1,0:T(8,128)} copy(f32[32768,6]{0,1:T(8,128)S(1)} %multiply_bitcast_fusion) | data formatting | bytes 1572864 | tf_op jit(solution)/shard_map/mul | solution.py:113
  74.0 41.2 %all_gather.6 = s32[32768,1]{0,1:T(1,128)S(1)} all-gather(s32[1024,1]{0,1:T(1,128)S(1)} %copy-done.13), channel_id=1, replica_groups=mesh['sec'=32,'depth'=4,'segment'=2] {'sec'}, dimensions={0}, use_global_device_ids=true | all-gather | bytes 135168 | tf_op jit(solution)/shard_map/all_gather | solution.py:106
  115.4 175.0 %scatter_fusion = f32[6,4096]{0,1:T(8,128)S(1)} fusion(f32[6,4096]{0,1:T(8,128)S(1)} %bitcast.378, s32[32768]{0:T(1024)S(1)} %bitcast.434, f32[32768,6]{1,0:T(8,128)} %copy.799), kind=kCustom, calls=%fused_computation.4 | custom fusion | flops 196608 | bytes 2490368 | tf_op jit(solution)/shard_map/scatter-add | solution.py:114
  292.5 7.4 %fusion.93 = (f32[1,1,2,16,128]{1,4,3,2,0:T(8,128)}, f32[1,1,2,16,128]{1,4,3,2,0:T(8,128)}, f32[1,1,2,16,128]{1,4,3,2,0:T(8,128)}, f32[1,1,2,16,128]{1,4,3,2,0:T...) fusion(f32[1,6,2,16,128]{1,4,3,2,0:T(8,128)S(1)} %bitcast.381), kind=kLoop, calls=%fused_computation.240 | loop fusion | bytes 196608 | tf_op jit(solution)/shard_map/slice | solution.py:62
  300.2 3.2 collective-permute-start.1
  305.6 4.6 collective-permute-start
  310.2 2.4 copy.866
  312.6 2.2 copy.865
  315.5 2.4 copy.871
  317.8 2.3 copy.870
  320.8 10.7 %fusion.3 = (f32[1,2,16,128]{3,2,1,0:T(8,128)S(1)}, f32[1,2,16,128]{3,2,1,0:T(8,128)S(1)}, pred[1,2,16,128]{3,2,1,0:T(8,128)(4,1)S(1)}, pred[1,2,16,128]{3,2,1,0...) fusion(f32[1,1,16,128]{3,2,1,0:T(8,128)S(1)} %slice.912, ...), kind=kLoop, calls=%fused_computation.29 | loop fusion | flops 233472 | bytes 229312 | tf_op jit(solution)/shard_map/add | solution.py:64
  332.2 3.2 bitcast_subtract_fusion
  335.4 7.0 %gather_fusion = f32[2048,3]{1,0:T(8,128)S(1)} fusion(f32[3,4096]{0,1:T(8,128)} %bitcast_subtract_fusion, s32[2048]{0:T(1024)S(1)} %get-tuple-element.103), kind=kCustom, calls=%fused_computation | custom fusion | bytes 57344 | tf_op jit(solution)/shard_map/gather | solution.py:53
  345.4 12.2 %scatter_fusion.1 = f32[3,4096]{0,1:T(8,128)S(1)} fusion(f32[3,4096]{0,1:T(8,128)S(1)} %copy.807, s32[2048]{0:T(1024)S(1)} %get-tuple-element.104, f32[2048,3]{1,0:T(8,128)S(1)} %copy.808), kind=kCustom, calls=%fused_computation.5 | custom fusion | flops 6144 | bytes 81920 | tf_op jit(solution)/shard_map/scatter-add | solution.py:55
  357.7 2.7 collective-permute-start.4
  360.5 3.9 fusion.92
  366.7 2.2 copy.876
  373.7 7.1 %collective-permute-done.3 = f32[1,3,1,16,128]{4,3,2,1,0:T(8,128)S(1)} collective-permute-done((f32[1,3,1,16,128]{4,3,2,1,0:T(8,128)S(1)}, f32[1,3,1,16,128]{4,3,2,1,0:T(8,128)S(1)}, u32[]{:S(2)}, u32[]{:S(2)}) %collective-permute-start.3) | collective-permute-done | bytes 24608 | tf_op jit(solution)/shard_map/ppermute | solution.py:13
  380.8 20.8 %multiply_add_fusion.6 = (f32[1,2,16,128]{3,2,1,0:T(8,128)S(1)}, f32[1,2,16,128]{3,2,1,0:T(8,128)S(1)}, f32[1,2,16,128]{3,2,1,0:T(8,128)S(1)}, f32[1,2,16,128]{3,2,1,0:T(8,128)S(1)}) fusion(f32[1,2,16,127]{3,2,1,0:T(8,128)S(1)} %slice.939, f32[1,1,2,16,128]{4,3,2,1,0:T(8,128)S(1)} %copy.875, f32[1,1,2,16,128]{4,3,2,1,0:T(8,128)S(1)} %copy.870, ...), kind=kLoop, calls=%fused_computation.178 | loop fusion | flops 307200 | bytes 245760 | tf_op jit(solution)/shard_map/add | solution.py:87
  401.6 3.1 collective-permute-start.6
  407.1 3.4 collective-permute-done.5
  412.8 3.2 sub.500
  415.9 7.2 %gather_fusion.1 = f32[2048,3]{1,0:T(8,128)S(1)} fusion(f32[3,4096]{0,1:T(8,128)} %sub.500, s32[2048]{0:T(1024)S(1)} %get-tuple-element.103), kind=kCustom, calls=%fused_computation.1 | custom fusion | bytes 57344 | tf_op jit(solution)/shard_map/gather | solution.py:53
  426.0 12.2 %scatter_fusion.2 = f32[3,4096]{0,1:T(8,128)S(1)} fusion(f32[3,4096]{0,1:T(8,128)S(1)} %copy-done, s32[2048]{0:T(1024)S(1)} %get-tuple-element.104, f32[2048,3]{1,0:T(8,128)S(1)} %copy.821), kind=kCustom, calls=%fused_computation.6 | custom fusion | flops 6144 | bytes 81920 | tf_op jit(solution)/shard_map/scatter-add | solution.py:55
  438.3 2.7 collective-permute-start.9
  441.1 3.9 fusion.91
  447.3 2.2 copy.883
  449.6 2.2 copy.881
  454.3 7.1 %collective-permute-done.8 = f32[1,3,1,16,128]{4,3,2,1,0:T(8,128)S(1)} collective-permute-done((f32[1,3,1,16,128]{4,3,2,1,0:T(8,128)S(1)}, f32[1,3,1,16,128]{4,3,2,1,0:T(8,128)S(1)}, u32[]{:S(2)}, u32[]{:S(2)}) %collective-permute-start.8) | collective-permute-done | bytes 24608 | tf_op jit(solution)/shard_map/ppermute | solution.py:13
  461.5 3.1 collective-permute-start.11
  467.0 3.4 collective-permute-done.10
  472.6 3.2 sub.519
  475.8 7.2 %gather_fusion.2 = f32[2048,3]{1,0:T(8,128)S(1)} fusion(f32[3,4096]{0,1:T(8,128)} %sub.519, s32[2048]{0:T(1024)S(1)} %get-tuple-element.103), kind=kCustom, calls=%fused_computation.2 | custom fusion | bytes 57344 | tf_op jit(solution)/shard_map/gather | solution.py:53
  485.9 12.2 %scatter_fusion.3 = f32[3,4096]{0,1:T(8,128)S(1)} fusion(f32[3,4096]{0,1:T(8,128)S(1)} %copy-done.1, s32[2048]{0:T(1024)S(1)} %get-tuple-element.104, f32[2048,3]{1,0:T(8,128)S(1)} %copy.834), kind=kCustom, calls=%fused_computation.7 | custom fusion | flops 6144 | bytes 81920 | tf_op jit(solution)/shard_map/scatter-add | solution.py:55
  498.2 2.8 collective-permute-start.14
  501.0 3.9 fusion.90
  507.2 2.2 copy.892
  509.5 2.2 copy.889
  514.2 7.1 %collective-permute-done.13 = f32[1,3,1,16,128]{4,3,2,1,0:T(8,128)S(1)} collective-permute-done((f32[1,3,1,16,128]{4,3,2,1,0:T(8,128)S(1)}, f32[1,3,1,16,128]{4,3,2,1,0:T(8,128)S(1)}, u32[]{:S(2)}, u32[]{:S(2)}) %collective-permute-start.13) | collective-permute-done | bytes 24608 | tf_op jit(solution)/shard_map/ppermute | solution.py:13
  521.4 3.1 collective-permute-start.16
  526.9 3.4 collective-permute-done.15
  532.5 3.2 sub.538
  535.7 7.2 %gather_fusion.3 = f32[2048,3]{1,0:T(8,128)S(1)} fusion(f32[3,4096]{0,1:T(8,128)} %sub.538, s32[2048]{0:T(1024)S(1)} %get-tuple-element.103), kind=kCustom, calls=%fused_computation.3 | custom fusion | bytes 57344 | tf_op jit(solution)/shard_map/gather | solution.py:53
  545.7 12.2 %scatter_fusion.4 = f32[3,4096]{0,1:T(8,128)S(1)} fusion(f32[3,4096]{0,1:T(8,128)S(1)} %copy-done.2, s32[2048]{0:T(1024)S(1)} %get-tuple-element.104, f32[2048,3]{1,0:T(8,128)S(1)} %copy.847), kind=kCustom, calls=%fused_computation.8 | custom fusion | flops 6144 | bytes 81920 | tf_op jit(solution)/shard_map/scatter-add | solution.py:55
  558.7 2.8 collective-permute-start.19
  564.2 6.6 %collective-permute-done.18 = f32[1,3,1,16,128]{4,3,2,1,0:T(8,128)S(1)} collective-permute-done((f32[1,3,1,16,128]{4,3,2,1,0:T(8,128)S(1)}, f32[1,3,1,16,128]{4,3,2,1,0:T(8,128)S(1)}, u32[]{:S(2)}, u32[]{:S(2)}) %collective-permute-start.18) | collective-permute-done | bytes 24608 | tf_op jit(solution)/shard_map/ppermute | solution.py:13
  (223 shorter events, 59.4 us)
Async XLA Ops:
  1.4 113.8 %all-to-all-start = ((s32[32,1,1024]{2,1,0:T(1,128)}), s32[32,1,1024]{2,1,0:T(1,128)S(1)}, u32[]{:S(2)}, u32[]{:S(2)}) async-start(s32[32,1,1024]{2,1,0:T(1,128)} %stack.180), calls=%async_computation | async-start | bytes 262144 | tf_op jit(solution)/shard_map/all_to_all | solution.py:108
  60.9 8.9 %slice-start = ((f32[1,9,2,16,128]{4,3,2,1,0:T(8,128)}), f32[1,6,2,16,128]{4,3,2,1,0:T(8,128)S(1)}, s32[]{:S(2)}) async-start(f32[1,9,2,16,128]{4,3,2,1,0:T(8,128)} %param.9), calls=%async_computation.1 | async-start | bytes 196608 | tf_op jit(solution)/shard_map/slice | solution.py:114
  69.8 0.7 copy-start.7
  69.8 1.4 slice-start.1
  69.8 3.4 copy-start.8
  69.8 4.1 copy-start.13
  69.8 45.3 %copy-start.12 = (s32[2048]{0:T(1024)S(1)}, s32[2048]{0:T(1024)}, u32[]{:S(2)}) copy-start(s32[2048]{0:T(1024)} %param.17) | copy-start | bytes 24580
  299.9 5.1 copy-start.5
  300.2 20.6 %collective-permute-start.1 = (f32[1,3,2,1,128]{4,3,2,1,0:T(1,128)S(1)}, f32[1,3,2,1,128]{4,3,2,1,0:T(1,128)S(1)}, u32[]{:S(2)}, u32[]{:S(2)}) collective-permute-start(f32[1,3,2,1,128]{4,3,2,1,0:T(1,128)S(1)} %pad_maximum_fusion.8), channel_id=1, source_target_pairs={{0,2},{2,4},{4,6},{1,3},{3,5},{5,7},{8,10},{10,12},{12,14},{9,11},... | collective-permute-start | bytes 9224 | tf_op jit(solution)/shard_map/ppermute | solution.py:13
  305.6 15.1 %collective-permute-start = (f32[1,3,1,16,128]{4,3,2,1,0:T(8,128)S(1)}, f32[1,3,1,16,128]{4,3,2,1,0:T(8,128)S(1)}, u32[]{:S(2)}, u32[]{:S(2)}) collective-permute-start(f32[1,3,1,16,128]{4,3,2,1,0:T(8,128)S(1)} %pad_maximum_fusion.4), channel_id=1, source_target_pairs={{0,8},{8,16},{16,24},{24,32},{32,40},{40,48},{48,56},{56,64},{64,7... | collective-permute-start | bytes 73736 | tf_op jit(solution)/shard_map/ppermute | solution.py:13
  310.2 4.6 copy-start.4
  315.5 4.6 copy-start.3
  317.8 2.9 copy-start.6
  317.8 2.9 copy-start.11
  332.2 12.0 %copy-start.9 = (f32[16]{0:T(128)S(1)}, f32[16]{0:T(128)}, u32[]{:S(2)}) copy-start(f32[16]{0:T(128)} %param.13) | copy-start | bytes 196
  342.8 2.2 collective-permute-start.2
  357.7 15.9 %collective-permute-start.4 = (f32[1,3,2,1,128]{4,2,3,1,0:T(2,128)S(1)}, f32[1,3,2,1,128]{4,2,3,1,0:T(2,128)S(1)}, u32[]{:S(2)}, u32[]{:S(2)}) collective-permute-start(f32[1,3,2,1,128]{4,2,3,1,0:T(2,128)S(1)} %copy.877), channel_id=1, source_target_pairs={{2,0},{4,2},{6,4},{3,1},{5,3},{7,5},{10,8},{12,10},{14,12},{11,9},... | collective-permute-start | bytes 9224 | tf_op jit(solution)/shard_map/ppermute | solution.py:13
  371.7 9.0 %collective-permute-start.3 = (f32[1,3,1,16,128]{4,3,2,1,0:T(8,128)S(1)}, f32[1,3,1,16,128]{4,3,2,1,0:T(8,128)S(1)}, u32[]{:S(2)}, u32[]{:S(2)}) collective-permute-start(f32[1,3,1,16,128]{4,3,2,1,0:T(8,128)S(1)} %copy.874), channel_id=1, source_target_pairs={{8,0},{16,8},{24,16},{32,24},{40,32},{48,40},{56,48},{64,56},{72,6... | collective-permute-start | bytes 73736 | tf_op jit(solution)/shard_map/ppermute | solution.py:13
  401.6 5.5 collective-permute-start.6
  404.8 5.7 collective-permute-start.5
  415.9 10.0 %copy-start = (f32[3,4096]{0,1:T(8,128)S(1)}, f32[3,4096]{0,1:T(8,128)}, u32[]{:S(2)}) copy-start(f32[3,4096]{0,1:T(8,128)} %copy.820) | copy-start | bytes 147460
  423.5 2.1 collective-permute-start.7
  438.3 16.0 %collective-permute-start.9 = (f32[1,3,2,1,128]{4,2,3,1,0:T(2,128)S(1)}, f32[1,3,2,1,128]{4,2,3,1,0:T(2,128)S(1)}, u32[]{:S(2)}, u32[]{:S(2)}) collective-permute-start(f32[1,3,2,1,128]{4,2,3,1,0:T(2,128)S(1)} %copy.885), channel_id=1, source_target_pairs={{2,0},{4,2},{6,4},{3,1},{5,3},{7,5},{10,8},{12,10},{14,12},{11,9},... | collective-permute-start | bytes 9224 | tf_op jit(solution)/shard_map/ppermute | solution.py:13
  452.4 9.0 %collective-permute-start.8 = (f32[1,3,1,16,128]{4,3,2,1,0:T(8,128)S(1)}, f32[1,3,1,16,128]{4,3,2,1,0:T(8,128)S(1)}, u32[]{:S(2)}, u32[]{:S(2)}) collective-permute-start(f32[1,3,1,16,128]{4,3,2,1,0:T(8,128)S(1)} %copy.882), channel_id=1, source_target_pairs={{8,0},{16,8},{24,16},{32,24},{40,32},{48,40},{56,48},{64,56},{72,6... | collective-permute-start | bytes 73736 | tf_op jit(solution)/shard_map/ppermute | solution.py:13
  461.5 5.5 collective-permute-start.11
  464.7 5.7 collective-permute-start.10
  475.8 10.0 %copy-start.1 = (f32[3,4096]{0,1:T(8,128)S(1)}, f32[3,4096]{0,1:T(8,128)}, u32[]{:S(2)}) copy-start(f32[3,4096]{0,1:T(8,128)} %copy.833) | copy-start | bytes 147460
  483.3 2.1 collective-permute-start.12
  498.2 16.0 %collective-permute-start.14 = (f32[1,3,2,1,128]{4,2,3,1,0:T(2,128)S(1)}, f32[1,3,2,1,128]{4,2,3,1,0:T(2,128)S(1)}, u32[]{:S(2)}, u32[]{:S(2)}) collective-permute-start(f32[1,3,2,1,128]{4,2,3,1,0:T(2,128)S(1)} %copy.893), channel_id=1, source_target_pairs={{2,0},{4,2},{6,4},{3,1},{5,3},{7,5},{10,8},{12,10},{14,12},{11,9},... | collective-permute-start | bytes 9224 | tf_op jit(solution)/shard_map/ppermute | solution.py:13
  512.2 9.0 %collective-permute-start.13 = (f32[1,3,1,16,128]{4,3,2,1,0:T(8,128)S(1)}, f32[1,3,1,16,128]{4,3,2,1,0:T(8,128)S(1)}, u32[]{:S(2)}, u32[]{:S(2)}) collective-permute-start(f32[1,3,1,16,128]{4,3,2,1,0:T(8,128)S(1)} %copy.890), channel_id=1, source_target_pairs={{8,0},{16,8},{24,16},{32,24},{40,32},{48,40},{56,48},{64,56},{72,6... | collective-permute-start | bytes 73736 | tf_op jit(solution)/shard_map/ppermute | solution.py:13
  521.4 5.5 collective-permute-start.16
  524.6 5.7 collective-permute-start.15
  535.7 10.0 %copy-start.2 = (f32[3,4096]{0,1:T(8,128)S(1)}, f32[3,4096]{0,1:T(8,128)}, u32[]{:S(2)}) copy-start(f32[3,4096]{0,1:T(8,128)} %copy.846) | copy-start | bytes 147460
  543.2 2.1 collective-permute-start.17
  558.7 5.5 collective-permute-start.19
  561.8 9.0 %collective-permute-start.18 = (f32[1,3,1,16,128]{4,3,2,1,0:T(8,128)S(1)}, f32[1,3,1,16,128]{4,3,2,1,0:T(8,128)S(1)}, u32[]{:S(2)}, u32[]{:S(2)}) collective-permute-start(f32[1,3,1,16,128]{4,3,2,1,0:T(8,128)S(1)} %slice.1059), channel_id=1, source_target_pairs={{8,0},{16,8},{24,16},{32,24},{40,32},{48,40},{56,48},{64,56},{72,6... | collective-permute-start | bytes 73736 | tf_op jit(solution)/shard_map/ppermute | solution.py:13
  570.9 0.7 copy-start.10
